TPU v7x, 32 devices: a whole 2x2x4 slice. The times are simulated.
32 devices in a mesh: groups: 2 (over y), ctx: 4 (over z), wt: 2 (over x), sub: 2 (over core).
Axes of the slice: x: 2, y: 2, z: 4, core: 2. Of those that a mesh axis runs over, the one named last changes fastest.
Arguments:
- queries: bfloat16 [16, 32, 128, 576], P(('groups', 'ctx'), None, ('wt', 'sub')), parts along dimension 0, may hold values from -80 to 80
- selection: int32 [16, 4, 2], P(('groups', 'ctx')), parts along dimension 0, may hold values from -1 to 15, as said below
- latent_cache: bfloat16 [128, 64, 576], P(('groups', 'ctx')), parts along dimension 0, may hold values from -8 to 8
- value_up: bfloat16 [128, 512, 128], P(None, ('wt', 'sub')), may hold values from -1 to 1
Outputs:
- attended: bfloat16 [16, 32, 128, 128], P(('groups', 'ctx'), None, ('wt', 'sub')), parts along dimension 0
There are 2 independent parts, one for each index of `groups`. A program takes and returns all parts, laid end to end along the dimension named above; an argument that names none is the same for every part. Nothing has to cross between parts.
Inputs may be any that keep to these rules, and one draw needn't show every extreme that they name: `selection`: entry [c, o, s] is the number of a block among the 16 of owner o, or -1 for an empty slot; in an owner's slots live entries come first and differ. Each query block has 4 live entries in all, and in every query block some owner fills all 2 slots.
All inputs are finite; a program needn't handle non-finite values.
Results may differ from a plain program's by a relative error of at most 0.008.
Values may be sent and summed in bfloat16 or wider, within the bound.
No kernel may reach another device: no remote copies, remote signals or barrier semaphores. Data moves between devices by JAX's collectives and lax.ppermute only.
A program may use at most 128 MiB of HBM per device.

v0:
```python
import jax
import jax.numpy as jnp
from jax import lax
from jax.sharding import PartitionSpec as P

LAT = 512
ROPE = 64
NOPE = 128


def attend(query, blocks, chosen):
    width = query.shape[2]
    owners = chosen.shape[0]
    count = chosen.shape[0] * chosen.shape[1]
    live = (chosen >= 0).reshape(-1)
    ranked = jnp.where(live, 0, count).astype(jnp.int32) + jnp.arange(count, dtype=jnp.int32)
    picked = jnp.argsort(ranked)[:owners]
    keys = blocks.reshape(count, blocks.shape[2], width)[picked].reshape(-1, width)
    rows = query.reshape(-1, width)
    scores = jnp.einsum("rd,kd->rk", rows, keys, preferred_element_type=jnp.float32)
    scores = scores * jnp.float32((NOPE + ROPE) ** (-0.5))
    expo = jnp.exp(scores - jnp.max(scores, axis=1, keepdims=True))
    totals = jnp.sum(expo, axis=1, keepdims=True)
    weights = expo.astype(jnp.bfloat16)
    latent = (jnp.dot(weights, keys[:, :LAT], preferred_element_type=jnp.float32) / totals).astype(
        jnp.bfloat16
    )
    return latent.reshape(query.shape[0], query.shape[1], LAT)


def per_device(queries, selection, latent_cache, value_up):
    owners = lax.axis_size("ctx")
    spans, per_span, heads_here, width = queries.shape
    slots = selection.shape[2]
    block_len = latent_cache.shape[1]

    def serve(asked):
        safe = jnp.clip(asked, 0, latent_cache.shape[0] - 1)
        return lax.all_to_all(latent_cache[safe], "ctx", split_axis=0, concat_axis=0, tiled=True)

    def fetch(wanted):
        half = slots // 2
        mine = lax.dynamic_slice_in_dim(wanted, lax.axis_index("sub") * half, half, 2)
        count = mine.shape[1] * mine.shape[2]
        fetched = serve(
            lax.all_to_all(
                mine.reshape(owners, count), "ctx", split_axis=0, concat_axis=0, tiled=True
            )
        )
        fetched = fetched.reshape(owners, mine.shape[1], mine.shape[2], block_len, width)
        fetched = lax.all_gather(fetched, "sub", axis=2, tiled=True)
        return fetched

    wanted_all = jnp.transpose(selection, (1, 0, 2))
    gathered = [fetch(wanted_all[:, index : index + 1])[:, 0] for index in range(spans)]
    latents = [attend(queries[index], gathered[index], selection[index]) for index in range(spans)]
    flat = jnp.stack(latents).reshape(spans * per_span, heads_here, LAT)
    my_weights = lax.all_to_all(value_up, ("wt", "sub"), split_axis=0, concat_axis=1, tiled=True)
    summed = jnp.einsum("nhl,hlv->nhv", flat, my_weights, preferred_element_type=jnp.float32)
    return summed.astype(jnp.bfloat16).reshape(spans, per_span, heads_here, my_weights.shape[2])


def solution(mesh):
    placed = (
        P(("groups", "ctx"), None, ("wt", "sub"), None),
        P(("groups", "ctx"), None, None),
        P(("groups", "ctx"), None, None),
        P(None, ("wt", "sub"), None),
    )
    return jax.shard_map(
        per_device,
        mesh=mesh,
        in_specs=placed,
        out_specs=P(("groups", "ctx"), None, ("wt", "sub"), None),
        check_vma=False,
    )
```

profile of v0, /device:TPU:0, one launch (start us, length us, event | category | flops | bytes accessed | tf_op | source)
XLA Modules:
  0.0 102.0 jit_solution(10457877809274622)
XLA Ops:
  0.0 0.9 copy.21
  0.9 0.7 constant_dynamic-slice_fusion.1
  1.6 6.3 %all-to-all-start = ((s32[4,1,1]{2,1,0:T(1,128)}), s32[4,1,1]{2,1,0:T(1,128)S(1)}, u32[]{:S(2)}, u32[]{:S(2)}) async-start(s32[4,1,1]{2,1,0:T(1,128)} %constant_dynamic-slice_fusion.1), calls=%async_computation | async-start | bytes 4096 | tf_op jit(solution)/shard_map/all_to_all | solution.py:46
  7.9 0.7 constant_dynamic-slice_fusion
  8.6 4.8 %all-to-all-done = s32[4,1,1]{2,1,0:T(1,128)S(1)} async-done(((s32[4,1,1]{2,1,0:T(1,128)}), s32[4,1,1]{2,1,0:T(1,128)S(1)}, u32[]{:S(2)}, u32[]{:S(2)}) %all-to-all-start) | async-done | bytes 48 | tf_op jit(solution)/shard_map/all_to_all | solution.py:46
  13.3 3.2 %all-to-all-start.2 = ((s32[4,1,1]{2,1,0:T(1,128)}), s32[4,1,1]{2,1,0:T(1,128)S(1)}, u32[]{:S(2)}, u32[]{:S(2)}) async-start(s32[4,1,1]{2,1,0:T(1,128)} %constant_dynamic-slice_fusion), calls=%async_computation.2 | async-start | bytes 4096 | tf_op jit(solution)/shard_map/all_to_all | solution.py:46
  16.7 1.3 %gather_fusion = bf16[4,64,576]{2,1,0:T(8,128)(2,1)} fusion(bf16[16,64,576]{2,1,0:T(8,128)(2,1)S(1)} %copy-done, s32[1024]{0:T(1024)S(1)} %pad_clamp_fusion.3), kind=kCustom, calls=%fused_computation | custom fusion | bytes 589840 | tf_op jit(solution)/shard_map/gather | solution.py:39
  18.0 4.0 %all-to-all-done.2 = s32[4,1,1]{2,1,0:T(1,128)S(1)} async-done(((s32[4,1,1]{2,1,0:T(1,128)}), s32[4,1,1]{2,1,0:T(1,128)S(1)}, u32[]{:S(2)}, u32[]{:S(2)}) %all-to-all-start.2) | async-done | bytes 48 | tf_op jit(solution)/shard_map/all_to_all | solution.py:46
  22.0 3.5 %all-to-all-start.1 = ((bf16[4,1,64,576]{3,2,1,0:T(8,128)(2,1)}), bf16[4,1,64,576]{3,2,1,0:T(8,128)(2,1)S(1)}, u32[]{:S(2)}, u32[]{:S(2)}) async-start(bf16[4,1,64,576]{3,2,1,0:T(8,128)(2,1)} %bitcast.1), calls=%async_computation.1 | async-start | bytes 655360 | tf_op jit(solution)/shard_map/all_to_all | solution.py:39
  25.7 1.3 %gather_fusion.2 = bf16[4,64,576]{2,1,0:T(8,128)(2,1)} fusion(bf16[16,64,576]{2,1,0:T(8,128)(2,1)S(1)} %copy-done, s32[1024]{0:T(1024)S(1)} %pad_clamp_fusion.1), kind=kCustom, calls=%fused_computation.2 | custom fusion | bytes 589840 | tf_op jit(solution)/shard_map/gather | solution.py:39
  27.0 5.8 %all-to-all-done.1 = bf16[4,1,64,576]{3,2,1,0:T(8,128)(2,1)S(1)} async-done(((bf16[4,1,64,576]{3,2,1,0:T(8,128)(2,1)}), bf16[4,1,64,576]{3,2,1,0:T(8,128)(2,1)S(1)}, u32[]{:S(2)}, u32[]{:S(2)}) %all-to-all-start.1) | async-done | bytes 294944 | tf_op jit(solution)/shard_map/all_to_all | solution.py:39
  32.8 3.6 %all-to-all-start.3 = ((bf16[4,1,64,576]{3,2,1,0:T(8,128)(2,1)}), bf16[4,1,64,576]{3,2,1,0:T(8,128)(2,1)S(1)}, u32[]{:S(2)}, u32[]{:S(2)}) async-start(bf16[4,1,64,576]{3,2,1,0:T(8,128)(2,1)} %bitcast.6), calls=%async_computation.3 | async-start | bytes 655360 | tf_op jit(solution)/shard_map/all_to_all | solution.py:39
  36.7 6.9 %all-to-all-done.3 = bf16[4,1,64,576]{3,2,1,0:T(8,128)(2,1)S(1)} async-done(((bf16[4,1,64,576]{3,2,1,0:T(8,128)(2,1)}), bf16[4,1,64,576]{3,2,1,0:T(8,128)(2,1)S(1)}, u32[]{:S(2)}, u32[]{:S(2)}) %all-to-all-start.3) | async-done | bytes 294944 | tf_op jit(solution)/shard_map/all_to_all | solution.py:39
  43.7 0.7 copy-done.2
  44.4 4.9 %all-to-all-start.4 = ((bf16[128,128,128]{2,1,0:T(8,128)(2,1)}), bf16[128,128,128]{2,1,0:T(8,128)(2,1)}, u32[]{:S(2)}, u32[]{:S(2)}) async-start(bf16[128,128,128]{2,1,0:T(8,128)(2,1)} %param.7), calls=%async_computation.4 | async-start | bytes 8388608 | tf_op jit(solution)/shard_map/all_to_all | solution.py:58
  49.3 1.0 sort.31
  50.2 1.0 sort.32
  51.3 3.1 %fusion.12 = (bf16[1,32,32,576]{3,2,1,0:T(8,128)(2,1)S(1)}, bf16[1,32,32,576]{3,2,1,0:T(8,128)(2,1)}) fusion(bf16[2,32,32,576]{3,2,1,0:T(8,128)(2,1)} %param.4), kind=kLoop, calls=%fused_computation.36 | loop fusion | bytes 4718592 | tf_op jit(solution)/shard_map/slice | solution.py:56
  54.4 2.3 %all-gather.1 = bf16[4,2,64,576]{3,2,1,0:T(8,128)(2,1)S(1)} all-gather(bf16[4,1,64,576]{3,2,1,0:T(8,128)(2,1)S(1)} %copy-done.3), channel_id=3, replica_groups=mesh['groups'=2,'ctx'=4,'wt'=2,'sub'=2] {'sub'}, dimensions={1}, use_global_device_ids=true | all-gather | bytes 884736 | tf_op jit(solution)/shard_map/all_gather | solution.py:51
  56.7 1.3 %gather_fusion.3 = bf16[4,64,576]{2,1,0:T(8,128)(2,1)} fusion(bf16[8,64,576]{2,1,0:T(8,128)(2,1)S(1)} %bitcast.30, s32[1024]{0:T(1024)S(1)} %pad_clamp_fusion), kind=kCustom, calls=%fused_computation.3 | custom fusion | bytes 589840 | tf_op jit(solution)/shard_map/gather | solution.py:18
  58.0 2.5 %all-gather = bf16[4,2,64,576]{3,2,1,0:T(8,128)(2,1)S(1)} all-gather(bf16[4,1,64,576]{3,2,1,0:T(8,128)(2,1)} %copy-done.1), channel_id=2, replica_groups=mesh['groups'=2,'ctx'=4,'wt'=2,'sub'=2] {'sub'}, dimensions={1}, use_global_device_ids=true | all-gather | bytes 884736 | tf_op jit(solution)/shard_map/all_gather | solution.py:51
  60.5 1.3 %gather_fusion.1 = bf16[4,64,576]{2,1,0:T(8,128)(2,1)} fusion(bf16[8,64,576]{2,1,0:T(8,128)(2,1)S(1)} %bitcast.31, s32[1024]{0:T(1024)S(1)} %pad_clamp_fusion.2), kind=kCustom, calls=%fused_computation.1 | custom fusion | bytes 589840 | tf_op jit(solution)/shard_map/gather | solution.py:18
  61.8 2.1 %fusion.14 = (f32[1024]{0:T(1024)S(1)}, f32[256,1024]{1,0:T(8,128)S(1)}) fusion(bf16[256,576]{1,0:T(8,128)(2,1)} %bitcast.32, bf16[1024,576]{1,0:T(8,128)(2,1)} %bitcast.28), kind=kOutput, calls=%fused_computation.38 | convolution fusion | flops 302513152 | bytes 2527232 | tf_op jit(solution)/shard_map/rd,kd->rk/dot_general | solution.py:20
  64.1 0.6 fusion.15
  65.0 0.5 divide_convert_fusion
  65.5 0.5 divide_convert_fusion.1
  66.1 0.2 pad_maximum_fusion
  66.3 1.2 %copy.24 = bf16[2,32,32,512]{3,1,0,2:T(8,128)(2,1)S(1)} copy(bf16[2,32,32,512]{3,2,1,0:T(8,128)(2,1)S(1)} %pad_maximum_fusion) | data formatting | bytes 4194304 | tf_op jit(solution)/shard_map/stack | solution.py:57
  67.4 30.0 %all-to-all-done.4 = bf16[128,128,128]{2,1,0:T(8,128)(2,1)} async-done(((bf16[128,128,128]{2,1,0:T(8,128)(2,1)}), bf16[128,128,128]{2,1,0:T(8,128)(2,1)}, u32[]{:S(2)}, u32[]{:S(2)}) %all-to-all-start.4) | async-done | bytes 4194336 | tf_op jit(solution)/shard_map/all_to_all | solution.py:58
  97.5 2.5 %copy.25 = bf16[4,32,128,128]{3,2,0,1:T(8,128)(2,1)S(1)} copy(bf16[4,32,128,128]{3,2,1,0:T(8,128)(2,1)} %bitcast.12) | data formatting | bytes 8388608 | tf_op jit(solution)/shard_map/all_to_all | solution.py:58
  100.0 0.9 convolution_convert_fusion
  100.8 1.1 %copy.26 = bf16[2,32,32,128]{3,2,1,0:T(8,128)(2,1)} copy(bf16[2,32,32,128]{3,1,0,2:T(8,128)(2,1)S(1)} %bitcast.29) | data formatting | bytes 1048576 | tf_op jit(solution)/shard_map/reshape | solution.py:60
  (33 shorter events, 1.3 us)
Async XLA Ops:
  0.0 16.7 %copy-start = (bf16[16,64,576]{2,1,0:T(8,128)(2,1)S(1)}, bf16[16,64,576]{2,1,0:T(8,128)(2,1)}, u32[]{:S(2)}) copy-start(bf16[16,64,576]{2,1,0:T(8,128)(2,1)} %param.6) | copy-start | bytes 3538948
  0.0 36.4 %copy-start.6 = (s32[2,4,2]{1,2,0:T(2,128)S(1)}, s32[2,4,2]{1,2,0:T(2,128)}, u32[]{:S(2)}) copy-start(s32[2,4,2]{1,2,0:T(2,128)} %param.5) | copy-start | bytes 196
  1.6 11.8 %all-to-all-start = ((s32[4,1,1]{2,1,0:T(1,128)}), s32[4,1,1]{2,1,0:T(1,128)S(1)}, u32[]{:S(2)}, u32[]{:S(2)}) async-start(s32[4,1,1]{2,1,0:T(1,128)} %constant_dynamic-slice_fusion.1), calls=%async_computation | async-start | bytes 4096 | tf_op jit(solution)/shard_map/all_to_all | solution.py:46
  13.3 8.7 %all-to-all-start.2 = ((s32[4,1,1]{2,1,0:T(1,128)}), s32[4,1,1]{2,1,0:T(1,128)S(1)}, u32[]{:S(2)}, u32[]{:S(2)}) async-start(s32[4,1,1]{2,1,0:T(1,128)} %constant_dynamic-slice_fusion), calls=%async_computation.2 | async-start | bytes 4096 | tf_op jit(solution)/shard_map/all_to_all | solution.py:46
  22.0 10.7 %all-to-all-start.1 = ((bf16[4,1,64,576]{3,2,1,0:T(8,128)(2,1)}), bf16[4,1,64,576]{3,2,1,0:T(8,128)(2,1)S(1)}, u32[]{:S(2)}, u32[]{:S(2)}) async-start(bf16[4,1,64,576]{3,2,1,0:T(8,128)(2,1)} %bitcast.1), calls=%async_computation.1 | async-start | bytes 655360 | tf_op jit(solution)/shard_map/all_to_all | solution.py:39
  32.8 10.9 %copy-start.1 = (bf16[4,1,64,576]{3,2,1,0:T(8,128)(2,1)}, bf16[4,1,64,576]{3,2,1,0:T(8,128)(2,1)S(1)}, u32[]{:S(2)}) copy-start(bf16[4,1,64,576]{3,2,1,0:T(8,128)(2,1)S(1)} %all-to-all-done.1) | copy-start | bytes 884740
  32.8 10.9 %all-to-all-start.3 = ((bf16[4,1,64,576]{3,2,1,0:T(8,128)(2,1)}), bf16[4,1,64,576]{3,2,1,0:T(8,128)(2,1)S(1)}, u32[]{:S(2)}, u32[]{:S(2)}) async-start(bf16[4,1,64,576]{3,2,1,0:T(8,128)(2,1)} %bitcast.6), calls=%async_computation.3 | async-start | bytes 655360 | tf_op jit(solution)/shard_map/all_to_all | solution.py:39
  43.7 0.7 copy-start.2
  44.4 53.1 %all-to-all-start.4 = ((bf16[128,128,128]{2,1,0:T(8,128)(2,1)}), bf16[128,128,128]{2,1,0:T(8,128)(2,1)}, u32[]{:S(2)}, u32[]{:S(2)}) async-start(bf16[128,128,128]{2,1,0:T(8,128)(2,1)} %param.7), calls=%async_computation.4 | async-start | bytes 8388608 | tf_op jit(solution)/shard_map/all_to_all | solution.py:58
  51.3 3.1 %copy-start.3 = (bf16[4,1,64,576]{3,2,1,0:T(8,128)(2,1)S(1)}, bf16[4,1,64,576]{3,2,1,0:T(8,128)(2,1)}, u32[]{:S(2)}) copy-start(bf16[4,1,64,576]{3,2,1,0:T(8,128)(2,1)} %copy-done.2) | copy-start | bytes 884740
  61.8 2.3 %copy-start.5 = (bf16[4,64,576]{2,1,0:T(8,128)(2,1)S(1)}, bf16[4,64,576]{2,1,0:T(8,128)(2,1)}, u32[]{:S(2)}) copy-start(bf16[4,64,576]{2,1,0:T(8,128)(2,1)} %gather_fusion.1) | copy-start | bytes 884740
  64.1 1.0 copy-start.4
where the time goes:
time: 103 us; the launch traced here: 102 us
  waiting for transfers between devices  51.5 us (50%)
  starting transfers between devices  21.5 us (21%)
  local copies, waits for them, and re-layouts  16.6 us (16%)
  blocking collectives  4.81 us (5%)
  matrix products  4.57 us (4%)
  other arithmetic  2.85 us (3%)
    all_to_all x1, waiting for transfers between devices, per_device(): lax.all_to_all(value_up, ('wt', 'sub'), split_axis=0, concat_axis=1, tile...  30 us
    all_to_all x2, waiting for transfers between devices, serve(): lax.all_to_all(latent_cache[safe], 'ctx', split_axis=0, concat_axis=0, ti...  12.7 us
    all_to_all x2, starting transfers between devices, fetch(): lax.all_to_all(mine.reshape(owners, count), 'ctx', split_axis=0, concat_a...  9.57 us
    all_to_all x2, waiting for transfers between devices, fetch(): lax.all_to_all(mine.reshape(owners, count), 'ctx', split_axis=0, concat_a...  8.76 us
    all_to_all x2, starting transfers between devices, serve(): lax.all_to_all(latent_cache[safe], 'ctx', split_axis=0, concat_axis=0, ti...  7.06 us
    all_to_all x1, starting transfers between devices, per_device(): lax.all_to_all(value_up, ('wt', 'sub'), split_axis=0, concat_axis=1, tile...  4.86 us
    all_gather x2, blocking collectives, fetch(): fetched = lax.all_gather(fetched, 'sub', axis=2, tiled=True)  4.81 us
    slice x1, local copies, waits for them, and re-layouts, per_device(): queries[index]  3.08 us
  transfers between devices with their start and end apart: 5, of which 5 were waited for; matrix products, arithmetic and copies ran while one was open for 17% of the time, Pallas kernels for 0%

commit v1 on v0

v1 whole, which is shorter than its diff:
```python
import jax
import jax.numpy as jnp
from jax import lax
from jax.experimental import pallas as pl
from jax.experimental.pallas import tpu as pltpu
from jax.sharding import PartitionSpec as P

LAT = 512
ROPE = 64
NOPE = 128
SCALE = (NOPE + ROPE) ** (-0.5)
AXES = ("groups", "ctx", "wt", "sub")


SMEM = pl.BlockSpec(memory_space=pltpu.SMEM)
VMEM = pl.BlockSpec(memory_space=pltpu.VMEM)
ANY = pl.BlockSpec(memory_space=pl.ANY)
HBM = pl.BlockSpec(memory_space=pltpu.HBM)


def hop(array, move, **names):
    axes = tuple(name for name in AXES if name in names)
    sizes = [names[name] for name in axes]
    total = 1
    for size in sizes:
        total *= size
    pairs = []
    for at in range(total):
        left, place = at, []
        for size in reversed(sizes):
            place.insert(0, left % size)
            left //= size
        flat = 0
        for size, index in zip(sizes, move(*place)):
            flat = flat * size + index
        pairs.append((at, flat))
    return lax.ppermute(array, axes, pairs)


def pick(asked, cache, spans, owners, mixed):
    steps = len(asked)

    def kernel(*refs):
        asked_refs, cache_ref, out_refs, sem = refs[:steps], refs[steps], refs[steps + 1 : -1], refs[-1]
        mine, slot = lax.axis_index("ctx"), lax.axis_index("sub")
        copies = []
        for entry in range(owners):
            away = entry if mixed else None
            for span in range(spans):
                if mixed:
                    which = away.bit_length()
                    at = away - (1 << (which - 1)) if which else 0
                    number = asked_refs[which][at * spans + span, slot, mine]
                    target = out_refs[entry].at[span]
                else:
                    number = asked_refs[0][entry * spans + span, slot, mine]
                    target = out_refs[0].at[entry, span]
                copies.append(
                    pltpu.make_async_copy(cache_ref.at[jnp.maximum(number, 0)], target, sem)
                )
        for copy in copies:
            copy.start()
        for copy in copies:
            copy.wait()

    block = cache.shape[1:]
    if mixed:
        shapes = [jax.ShapeDtypeStruct((spans,) + block, cache.dtype)] * owners
    else:
        shapes = [jax.ShapeDtypeStruct((owners, spans) + block, cache.dtype)]
    return pl.pallas_call(
        kernel,
        out_shape=shapes,
        in_specs=[SMEM] * steps + [ANY],
        out_specs=[VMEM] * len(shapes),
        scratch_shapes=[pltpu.SemaphoreType.DMA],
        compiler_params=pltpu.CompilerParams(vmem_limit_bytes=16 << 20),
        name="pick",
    )(*asked, cache)


def weight_pieces(value_up, heads):
    groups, ctx, wide, subs = (lax.axis_size(name) for name in AXES)
    group, at, wt, sub = (lax.axis_index(name) for name in AXES)
    pieces, rules = [value_up], [lambda g, c, w, s: ((w * subs + s) * heads, w * subs + s, 0, heads)]

    def cut(chip, core, start, count):
        return lax.dynamic_slice_in_dim(value_up, (chip * subs + core) * heads + start, count, 0)

    square = groups == 2 and subs == 2 and ctx % 2 == 0
    half = heads // 2
    for step in range(1, wide):
        far = (wt + step) % wide
        sizes = dict(groups=groups, wt=wide, sub=subs)
        if square:
            first = hop(
                cut(far, sub ^ group, at % 2 * half, half),
                lambda g, w, s: (g, (w + step) % wide, s ^ g),
                **sizes,
            )
            last = hop(
                cut(far, sub ^ group ^ 1, (1 - at % 2) * half, half),
                lambda g, w, s: (g, (w + step) % wide, s ^ g ^ 1),
                **sizes,
            )
            side = hop(first, lambda g: (g ^ 1,), groups=groups)
            over = hop(first, lambda c: (c ^ 1,), ctx=ctx)
            for piece, across, along in ((first, 0, 0), (side, 1, 0), (over, 0, 1), (last, 1, 1)):
                pieces.append(piece)
                rules.append(
                    lambda g, c, w, s, step=step, across=across, along=along: (
                        0,
                        (w - step) % wide * subs + (s ^ g ^ across),
                        (c % 2 ^ along) * half,
                        half,
                    )
                )
        else:
            for twist in range(subs):
                piece = hop(
                    cut(far, (sub + twist) % subs, 0, heads),
                    lambda g, w, s: (g, (w + step) % wide, (s + twist) % subs),
                    **sizes,
                )
                pieces.append(piece)
                rules.append(
                    lambda g, c, w, s, step=step, twist=twist: (
                        0,
                        (w - step) % wide * subs + (s - twist) % subs,
                        0,
                        heads,
                    )
                )
    for step in range(1, subs):
        pieces.append(
            hop(cut(wt, (sub + step) % subs, 0, heads), lambda s: ((s + step) % subs,), sub=subs)
        )
        rules.append(
            lambda g, c, w, s, step=step: (0, w * subs + (s - step) % subs, 0, heads)
        )
    return pieces, rules


def attend(selection, query, mine, other, pieces, rules, mixed):
    heads, spans, per_span, width = query.shape
    slots, owners = selection.shape[1:]
    block = mine[0].shape[-2]
    rows, values = pieces[0].shape[1:]
    tokens = spans * per_span
    chunks = 2
    group = heads // chunks
    parts, landed = len(pieces), len(mine)

    def kernel(chosen_ref, query_ref, *refs):
        mine_refs, other_refs = refs[:landed], refs[landed : 2 * landed]
        piece_refs, out_ref = refs[2 * landed : 2 * landed + parts], refs[2 * landed + parts]
        keys, latent, weights, summed, result, weight_sem, out_sem = refs[2 * landed + parts + 1 :]
        place = [lax.axis_index(name) for name in AXES]
        arrivals = []
        for piece, rule in zip(piece_refs, rules):
            head_from, number, head_to, count = rule(*place)
            row_at = pl.multiple_of(number * rows, rows)
            arrivals.append(
                pltpu.make_async_copy(
                    piece.at[pl.ds(head_from, count)],
                    weights.at[pl.ds(head_to, count), pl.ds(row_at, rows)],
                    weight_sem,
                )
            )
        for copy in arrivals:
            copy.start()

        at, sub = place[1], place[3]
        for span in range(spans):
            filled = jnp.int32(0)
            for entry in range(owners):
                owner = at ^ entry if mixed else entry
                if mixed:
                    own, across = mine_refs[entry].at[span], other_refs[entry].at[span]
                else:
                    own, across = mine_refs[0].at[entry, span], other_refs[0].at[entry, span]
                for slot in range(slots):
                    live = chosen_ref[span, slot, owner] >= 0
                    here = sub == slot
                    start = pl.multiple_of(jnp.minimum(filled, owners - 1) * block, block)

                    @pl.when(jnp.logical_and(live, here))
                    def _():
                        keys[span, pl.ds(start, block), :] = own[...]

                    @pl.when(jnp.logical_and(live, jnp.logical_not(here)))
                    def _():
                        keys[span, pl.ds(start, block), :] = across[...]

                    filled = filled + live.astype(jnp.int32)

        def score(step):
            span, first = step % spans, step // spans * group
            lines = query_ref[first : first + group, span].reshape(group * per_span, width)
            return lax.dot_general(
                lines, keys[span], (((1,), (1,)), ((), ())), preferred_element_type=jnp.float32
            )

        def soften(scores):
            top = jnp.max(scores, axis=1, keepdims=True)
            expo = jnp.exp((scores - top) * jnp.float32(SCALE))
            return expo.astype(jnp.bfloat16), 1.0 / jnp.sum(expo, axis=1, keepdims=True)

        def gather(step, expo, inverse):
            span, first = step % spans, step // spans * group
            mixed_rows = jnp.dot(expo, keys[span, :, :LAT], preferred_element_type=jnp.float32)
            latent[first : first + group, span] = (
                (mixed_rows * inverse).astype(jnp.bfloat16).reshape(group, per_span, LAT)
            )

        steps = chunks * spans
        scores = {step: score(step) for step in range(min(2, steps))}
        soft = {0: soften(scores.pop(0))}
        for step in range(steps):
            if step + 2 < steps:
                scores[step + 2] = score(step + 2)
            if step + 1 < steps:
                soft[step + 1] = soften(scores.pop(step + 1))
            gather(step, *soft.pop(step))

        for copy in arrivals:
            copy.wait()
        departures = []
        for first in range(0, heads, 16):
            for head in range(first, first + 16):
                lines = latent[head].reshape(tokens, LAT)
                summed[pl.ds(head, tokens, stride=heads), :] = jnp.dot(
                    lines, weights[head], preferred_element_type=jnp.float32
                )
            whole = summed[...].reshape(tokens, heads, values)[:, first : first + 16]
            result[:, :, first : first + 16] = whole.astype(jnp.bfloat16).reshape(
                spans, per_span, 16, values
            )
            departures.append(
                pltpu.make_async_copy(
                    result.at[:, :, pl.ds(first, 16)], out_ref.at[:, :, pl.ds(first, 16)], out_sem
                )
            )
            departures[-1].start()
        for copy in departures:
            copy.wait()

    return pl.pallas_call(
        kernel,
        out_shape=jax.ShapeDtypeStruct((spans, per_span, heads, values), jnp.bfloat16),
        in_specs=[SMEM] + [VMEM] * (1 + 2 * landed) + [HBM] + [ANY] * (parts - 1),
        out_specs=ANY,
        scratch_shapes=[
            pltpu.VMEM((spans, owners * block, width), jnp.bfloat16),
            pltpu.VMEM((heads, spans, per_span, LAT), jnp.bfloat16),
            pltpu.VMEM((heads, LAT, values), jnp.bfloat16),
            pltpu.VMEM((tokens * heads, values), jnp.float32),
            pltpu.VMEM((spans, per_span, heads, values), jnp.bfloat16),
            pltpu.SemaphoreType.DMA,
            pltpu.SemaphoreType.DMA,
        ],
        compiler_params=pltpu.CompilerParams(vmem_limit_bytes=(24 if mixed else 44) << 20),
        name="attend",
    )(selection, query, *mine, *other, *pieces)


def per_device(queries, selection, latent_cache, value_up):
    owners, subs = lax.axis_size("ctx"), lax.axis_size("sub")
    spans, _, heads, _ = queries.shape
    chosen = jnp.transpose(selection, (0, 2, 1))
    mixed = owners <= 8

    asked = [chosen]
    while (1 << (len(asked) - 1)) < owners:
        step = 1 << (len(asked) - 1)
        whole = jnp.concatenate(asked) if len(asked) > 1 else chosen
        asked.append(hop(whole, lambda c: (c ^ step,), ctx=owners))
    if not mixed:
        order = jnp.arange(owners) ^ lax.axis_index("ctx")
        whole = jnp.concatenate(asked).reshape((owners,) + chosen.shape)[order]
        asked = [whole.reshape((owners * spans,) + chosen.shape[1:])]
    picked = pick(asked, latent_cache, spans, owners, mixed)
    if mixed:
        mine = [None] * owners
        for entry in sorted(range(owners), key=lambda e: (e == 0, e == 1, e)):
            got = picked[entry]
            if entry:
                got = hop(got, lambda c: (c ^ entry,), ctx=owners)
            mine[entry] = got
    else:
        mine = [lax.all_to_all(picked[0], "ctx", split_axis=0, concat_axis=0, tiled=True)]
    other = []
    for entry, piece in enumerate(mine):
        other.append(hop(piece, lambda s: (s ^ 1,), sub=subs))
    pieces, rules = weight_pieces(value_up, heads)
    query = jnp.transpose(queries, (2, 0, 1, 3))
    return attend(chosen, query, mine, other, pieces, rules, mixed)


def solution(mesh):
    placed = (
        P(("groups", "ctx"), None, ("wt", "sub"), None),
        P(("groups", "ctx"), None, None),
        P(("groups", "ctx"), None, None),
        P(None, ("wt", "sub"), None),
    )

    return jax.shard_map(
        per_device,
        mesh=mesh,
        in_specs=placed,
        out_specs=P(("groups", "ctx"), None, ("wt", "sub"), None),
        check_vma=False,
    )
```

time: 103 us -> 51.2 us (0.50)
  waiting for transfers between devices: 51.5 us -> 24.8 us
  local copies, waits for them, and re-layouts: 16.6 us -> 5.48 us
  starting transfers between devices: 21.5 us -> 13.9 us
  Pallas kernels: 0 us -> 6.69 us
  blocking collectives: 4.81 us -> 0 us
  matrix products: 4.57 us -> 0 us
  other arithmetic: 2.85 us -> 0.01 us
    all_to_all x5 -> x0, waiting for transfers between devices: 51.5 us -> none  [the longest x1 30 us: per_device(): lax.all_to_all(value_up, ('wt', 'sub'), split_axis=0, concat_axis=1, tile...]
    ppermute x0 -> x14, waiting for transfers between devices: none -> 24.8 us  [hop(): return lax.ppermute(array, axes, pairs)]
    all_to_all x5 -> x0, starting transfers between devices: 21.5 us -> none  [the longest x2 9.57 us: fetch(): lax.all_to_all(mine.reshape(owners, count), 'ctx', split_axis=0, concat_a...]
    ppermute x0 -> x14, starting transfers between devices: none -> 13.9 us  [hop(): return lax.ppermute(array, axes, pairs)]
    pallas_call x0 -> x2, Pallas kernels: none -> 6.69 us  [the longest x1 5.16 us: attend(): pl.pallas_call(kernel, out_shape=jax.ShapeDtypeStruct((spans, per_span, h...]
    gather x4 -> x0, local copies, waits for them, and re-layouts: 5.26 us -> none  [the longest x2 2.64 us: attend(): blocks.reshape(count, blocks.shape[2], width)[picked].reshape(-1, width)]
    all_gather x2 -> x0, blocking collectives: 4.81 us -> none  [fetch(): fetched = lax.all_gather(fetched, 'sub', axis=2, tiled=True)]
    dot_general x5 -> x0, matrix products: 4.57 us -> none  [the longest x2 2.71 us: attend(): jnp.einsum('rd,kd->rk', rows, keys, preferred_element_type=jnp.float32)]
  transfers between devices with their start and end apart: 5 -> 14, of which waited for: 5 -> 9; matrix products, arithmetic and copies ran while one was open for 17% -> 8% of each run, Pallas kernels for 0% -> 3%
where the time goes in v1:
time: 51.2 us; the launch traced here: 51 us
  waiting for transfers between devices  24.8 us (48%)
  starting transfers between devices  13.9 us (27%)
  Pallas kernels  6.69 us (13%)
  local copies, waits for them, and re-layouts  5.48 us (11%)
    ppermute x14, waiting for transfers between devices, hop(): return lax.ppermute(array, axes, pairs)  24.8 us
    ppermute x14, starting transfers between devices, hop(): return lax.ppermute(array, axes, pairs)  13.9 us
    pallas_call x1, Pallas kernels, attend(): pl.pallas_call(kernel, out_shape=jax.ShapeDtypeStruct((spans, per_span, h...  5.16 us
    dynamic_slice x2, local copies, waits for them, and re-layouts, cut(): lax.dynamic_slice_in_dim(value_up, (chip * subs + core) * heads + start,...  2.85 us
    unnamed x7, local copies, waits for them, and re-layouts  2.63 us
    pallas_call x1, Pallas kernels, pick(): pl.pallas_call(kernel, out_shape=shapes, in_specs=[SMEM] * steps + [ANY],...  1.54 us
  transfers between devices with their start and end apart: 14, of which 9 were waited for; matrix products, arithmetic and copies ran while one was open for 8% of the time, Pallas kernels for 3%

profile of v1, /device:TPU:0, one launch (start us, length us, event | category | flops | bytes accessed | tf_op | source)
XLA Modules:
  0.0 51.0 jit_solution(17624089621333851573)
XLA Ops:
  0.0 1.4 %constant_dynamic-slice_fusion.1 = (bf16[16,128,128]{2,1,0:T(8,128)(2,1)S(1)}, bf16[16,128,128]{2,1,0:T(8,128)(2,1)S(1)}) fusion(bf16[128,128,128]{2,1,0:T(8,128)(2,1)} %refs_8_.1, s32[]{:T(128)S(6)} %select_n.29, s32[]{:T(128)S(6)} %select_n.28), kind=kLoop, calls=%fused_computation.3 | loop fusion | bytes 2097160 | tf_op jit(solution)/shard_map/dynamic_slice | solution.py:88
  1.4 3.0 %collective-permute-start.9 = (bf16[16,128,128]{2,1,0:T(8,128)(2,1)S(1)}, bf16[16,128,128]{2,1,0:T(8,128)(2,1)S(1)}, u32[]{:S(2)}, u32[]{:S(2)}) collective-permute-start(bf16[16,128,128]{2,1,0:T(8,128)(2,1)S(1)} %get-tuple-element.14), channel_id=1, source_target_pairs={{0,2},{1,3},{2,0},{3,1},{16,19},{17,18},{18,17},{19,16},{4,6},{5,7... | collective-permute-start | bytes 1572872 | tf_op jit(solution)/shard_map/ppermute | solution.py:37
  4.4 1.5 %constant_dynamic-slice_fusion = bf16[32,128,128]{2,1,0:T(8,128)(2,1)S(1)} fusion(bf16[128,128,128]{2,1,0:T(8,128)(2,1)} %refs_8_.1, s32[]{:T(128)S(6)} %select_n.31), kind=kLoop, calls=%fused_computation.2 | loop fusion | bytes 2097156 | tf_op jit(solution)/shard_map/dynamic_slice | solution.py:88
  5.9 0.1 collective-permute-start.13
  6.0 1.6 %collective-permute-start = (s32[2,2,4]{2,1,0:T(2,128)S(1)}, s32[2,2,4]{2,1,0:T(2,128)S(1)}, u32[]{:S(2)}, u32[]{:S(2)}) collective-permute-start(s32[2,2,4]{2,1,0:T(2,128)S(1)} %bitcast.5), channel_id=1, source_target_pairs={{0,4},{4,0},{8,12},{12,8},{1,5},{5,1},{9,13},{13,9},{2,6},{6,2},{1... | collective-permute-start | bytes 200 | tf_op jit(solution)/shard_map/ppermute | solution.py:37
  7.6 2.0 %collective-permute-done.refs_1_ = s32[2,2,4]{2,1,0:T(2,128)S(1)} collective-permute-done((s32[2,2,4]{2,1,0:T(2,128)S(1)}, s32[2,2,4]{2,1,0:T(2,128)S(1)}, u32[]{:S(2)}, u32[]{:S(2)}) %collective-permute-start) | collective-permute-done | bytes 96 | tf_op jit(solution)/shard_map/ppermute | solution.py:37
  9.6 2.6 %collective-permute-start.1 = (s32[4,2,4]{2,1,0:T(2,128)S(1)}, s32[4,2,4]{2,1,0:T(2,128)S(1)}, u32[]{:S(2)}, u32[]{:S(2)}) collective-permute-start(s32[4,2,4]{2,1,0:T(2,128)S(1)} %pad_add_fusion), channel_id=1, source_target_pairs={{0,8},{4,12},{8,0},{12,4},{1,9},{5,13},{9,1},{13,5},{2,10},{6,14},... | collective-permute-start | bytes 392 | tf_op jit(solution)/shard_map/ppermute | solution.py:37
  12.2 1.9 %collective-permute-done.1.refs_2_ = s32[4,2,4]{2,1,0:T(2,128)S(1)} collective-permute-done((s32[4,2,4]{2,1,0:T(2,128)S(1)}, s32[4,2,4]{2,1,0:T(2,128)S(1)}, u32[]{:S(2)}, u32[]{:S(2)}) %collective-permute-start.1) | collective-permute-done | bytes 160 | tf_op jit(solution)/shard_map/ppermute | solution.py:37
  14.2 1.5 %pick.1 = (bf16[2,64,576]{2,1,0:T(8,128)(2,1)S(1)}, bf16[2,64,576]{2,1,0:T(8,128)(2,1)S(1)}, bf16[2,64,576]{2,1,0:T(8,128)(2,1)S(1)}, bf16[2,64,576]{2,1,0:T(8,128)(2,1)S(1)}) custom-call(s32[2,2,4]{2,1,0:T(2,128)S(1)} %bitcast.7, s32[2,2,4]{2,1,0:T(2,128)S(1)} %collective-permute-done.refs_1_, s32[4,2,4]{2,1,0:T(2,128)S(1)} %collective-permute-done.1.refs_2_, ...), custom_call_target="tpu_custom_call" | custom-call | tf_op jit(solution)/shard_map/pick/pallas_call | solution.py:71
  15.7 1.6 %collective-permute-start.2 = (bf16[2,64,576]{2,1,0:T(8,128)(2,1)S(1)}, bf16[2,64,576]{2,1,0:T(8,128)(2,1)S(1)}, u32[]{:S(2)}, u32[]{:S(2)}) collective-permute-start(bf16[2,64,576]{2,1,0:T(8,128)(2,1)S(1)} %get-tuple-element.10), channel_id=1, source_target_pairs={{0,4},{4,0},{8,12},{12,8},{1,5},{5,1},{9,13},{13,9},{2,6},{6,2},{1... | collective-permute-start | bytes 442376 | tf_op jit(solution)/shard_map/ppermute | solution.py:37
  17.3 2.6 %collective-permute-start.3 = (bf16[2,64,576]{2,1,0:T(8,128)(2,1)S(1)}, bf16[2,64,576]{2,1,0:T(8,128)(2,1)S(1)}, u32[]{:S(2)}, u32[]{:S(2)}) collective-permute-start(bf16[2,64,576]{2,1,0:T(8,128)(2,1)S(1)} %get-tuple-element.11), channel_id=1, source_target_pairs={{0,8},{4,12},{8,0},{12,4},{1,9},{5,13},{9,1},{13,5},{2,10},{6,14},... | collective-permute-start | bytes 442376 | tf_op jit(solution)/shard_map/ppermute | solution.py:37
  19.9 0.2 collective-permute-start.4
  20.2 2.6 %collective-permute-done.2.refs_1_ = bf16[2,64,576]{2,1,0:T(8,128)(2,1)S(1)} collective-permute-done((bf16[2,64,576]{2,1,0:T(8,128)(2,1)S(1)}, bf16[2,64,576]{2,1,0:T(8,128)(2,1)S(1)}, u32[]{:S(2)}, u32[]{:S(2)}) %collective-permute-start.2) | collective-permute-done | bytes 147488 | tf_op jit(solution)/shard_map/ppermute | solution.py:37
  22.7 0.0 collective-permute-start.5
  22.7 8.5 %collective-permute-done.3.refs_2_ = bf16[2,64,576]{2,1,0:T(8,128)(2,1)S(1)} collective-permute-done((bf16[2,64,576]{2,1,0:T(8,128)(2,1)S(1)}, bf16[2,64,576]{2,1,0:T(8,128)(2,1)S(1)}, u32[]{:S(2)}, u32[]{:S(2)}) %collective-permute-start.3) | collective-permute-done | bytes 147488 | tf_op jit(solution)/shard_map/ppermute | solution.py:37
  31.3 0.0 collective-permute-start.12
  31.3 0.0 collective-permute-done.9.refs_9_
  31.3 0.0 collective-permute-start.11
  31.3 0.0 collective-permute-done.4.refs_3_
  31.3 1.8 %collective-permute-start.10 = (bf16[16,128,128]{2,1,0:T(8,128)(2,1)S(1)}, bf16[16,128,128]{2,1,0:T(8,128)(2,1)S(1)}, u32[]{:S(2)}, u32[]{:S(2)}) collective-permute-start(bf16[16,128,128]{2,1,0:T(8,128)(2,1)S(1)} %collective-permute-done.9.refs_9_), channel_id=1, source_target_pairs={{0,16},{16,0},{1,17},{17,1},{2,18},{18,2},{3,19},{19,3},{4,20},{20... | collective-permute-start | bytes 1572872 | tf_op jit(solution)/shard_map/ppermute | solution.py:37
  33.1 0.0 collective-permute-done.5.refs_4_
  33.1 0.0 collective-permute-start.6
  33.1 1.4 %collective-permute-done.6.refs_5_ = bf16[2,64,576]{2,1,0:T(8,128)(2,1)S(1)} collective-permute-done((bf16[2,64,576]{2,1,0:T(8,128)(2,1)S(1)}, bf16[2,64,576]{2,1,0:T(8,128)(2,1)S(1)}, u32[]{:S(2)}, u32[]{:S(2)}) %collective-permute-start.6) | collective-permute-done | bytes 147488 | tf_op jit(solution)/shard_map/ppermute | solution.py:37
  34.5 0.1 collective-permute-start.7
  34.7 1.3 %collective-permute-done.7.refs_6_ = bf16[2,64,576]{2,1,0:T(8,128)(2,1)S(1)} collective-permute-done((bf16[2,64,576]{2,1,0:T(8,128)(2,1)S(1)}, bf16[2,64,576]{2,1,0:T(8,128)(2,1)S(1)}, u32[]{:S(2)}, u32[]{:S(2)}) %collective-permute-start.7) | collective-permute-done | bytes 147488 | tf_op jit(solution)/shard_map/ppermute | solution.py:37
  35.9 0.1 collective-permute-start.8
  36.1 2.6 %copy.7 = bf16[2,32,32,576]{3,1,0,2:T(8,128)(2,1)S(1)} copy(bf16[2,32,32,576]{3,2,1,0:T(8,128)(2,1)} %param.4) | data formatting | bytes 4718592 | tf_op args[0]
  38.7 5.9 %collective-permute-done.12.refs_12_ = bf16[16,128,128]{2,1,0:T(8,128)(2,1)S(1)} collective-permute-done((bf16[16,128,128]{2,1,0:T(8,128)(2,1)S(1)}, bf16[16,128,128]{2,1,0:T(8,128)(2,1)S(1)}, u32[]{:S(2)}, u32[]{:S(2)}) %collective-permute-start.12) | collective-permute-done | bytes 524320 | tf_op jit(solution)/shard_map/ppermute | solution.py:37
  44.6 1.2 %collective-permute-done.11.refs_11_ = bf16[16,128,128]{2,1,0:T(8,128)(2,1)S(1)} collective-permute-done((bf16[16,128,128]{2,1,0:T(8,128)(2,1)S(1)}, bf16[16,128,128]{2,1,0:T(8,128)(2,1)S(1)}, u32[]{:S(2)}, u32[]{:S(2)}) %collective-permute-start.11) | collective-permute-done | bytes 524320 | tf_op jit(solution)/shard_map/ppermute | solution.py:37
  45.8 0.1 collective-permute-done.10.refs_10_
  45.8 0.0 collective-permute-done.13.refs_13_
  45.8 5.2 %attend.1 = bf16[2,32,32,128]{3,2,1,0:T(8,128)(2,1)} custom-call(s32[2,2,4]{2,1,0:T(2,128)S(1)} %bitcast.8, bf16[32,2,32,576]{3,2,1,0:T(8,128)(2,1)S(1)} %bitcast.4, bf16[2,64,576]{2,1,0:T(8,128)(2,1)S(1)} %get-tuple-element.9.refs_0_, bf16[2,64,576]{2,1,0:T(8,128)(2,1)S(1)} %collective-permute-done.2.refs_1_, ...), custom_call_target="tpu_custom_call" | custom-call | tf_op jit(solution)/shard_map/attend/pallas_call | solution.py:248
  (8 shorter events, 0.0 us)
Async XLA Ops:
  0.0 6.0 %copy-start.2 = (s32[2,4,2]{1,2,0:T(2,128)S(1)}, s32[2,4,2]{1,2,0:T(2,128)}, u32[]{:S(2)}) copy-start(s32[2,4,2]{1,2,0:T(2,128)} %param.5) | copy-start | bytes 196
  0.0 14.2 %copy-start.1 = (bf16[16,64,576]{2,1,0:T(8,128)(2,1)S(1)}, bf16[16,64,576]{2,1,0:T(8,128)(2,1)}, u32[]{:S(2)}) copy-start(bf16[16,64,576]{2,1,0:T(8,128)(2,1)} %refs_3_.1) | copy-start | bytes 3538948
  1.4 29.9 %collective-permute-start.9 = (bf16[16,128,128]{2,1,0:T(8,128)(2,1)S(1)}, bf16[16,128,128]{2,1,0:T(8,128)(2,1)S(1)}, u32[]{:S(2)}, u32[]{:S(2)}) collective-permute-start(bf16[16,128,128]{2,1,0:T(8,128)(2,1)S(1)} %get-tuple-element.14), channel_id=1, source_target_pairs={{0,2},{1,3},{2,0},{3,1},{16,19},{17,18},{18,17},{19,16},{4,6},{5,7... | collective-permute-start | bytes 1572872 | tf_op jit(solution)/shard_map/ppermute | solution.py:37
  4.4 41.4 %copy-start = (bf16[128,128,128]{2,1,0:T(8,128)(2,1)S(1)}, bf16[128,128,128]{2,1,0:T(8,128)(2,1)}, u32[]{:S(2)}) copy-start(bf16[128,128,128]{2,1,0:T(8,128)(2,1)} %refs_8_.1) | copy-start | bytes 12582916
  5.9 39.9 %collective-permute-start.13 = (bf16[32,128,128]{2,1,0:T(8,128)(2,1)S(1)}, bf16[32,128,128]{2,1,0:T(8,128)(2,1)S(1)}, u32[]{:S(2)}, u32[]{:S(2)}) collective-permute-start(bf16[32,128,128]{2,1,0:T(8,128)(2,1)S(1)} %constant_dynamic-slice_fusion), channel_id=1, source_target_pairs={{0,1},{1,0},{2,3},{3,2},{4,5},{5,4},{6,7},{7,6},{8,9},{9,8},{10,11... | collective-permute-start | bytes 3145736 | tf_op jit(solution)/shard_map/ppermute | solution.py:37
  6.0 3.7 %collective-permute-start = (s32[2,2,4]{2,1,0:T(2,128)S(1)}, s32[2,2,4]{2,1,0:T(2,128)S(1)}, u32[]{:S(2)}, u32[]{:S(2)}) collective-permute-start(s32[2,2,4]{2,1,0:T(2,128)S(1)} %bitcast.5), channel_id=1, source_target_pairs={{0,4},{4,0},{8,12},{12,8},{1,5},{5,1},{9,13},{13,9},{2,6},{6,2},{1... | collective-permute-start | bytes 200 | tf_op jit(solution)/shard_map/ppermute | solution.py:37
  9.6 4.5 %collective-permute-start.1 = (s32[4,2,4]{2,1,0:T(2,128)S(1)}, s32[4,2,4]{2,1,0:T(2,128)S(1)}, u32[]{:S(2)}, u32[]{:S(2)}) collective-permute-start(s32[4,2,4]{2,1,0:T(2,128)S(1)} %pad_add_fusion), channel_id=1, source_target_pairs={{0,8},{4,12},{8,0},{12,4},{1,9},{5,13},{9,1},{13,5},{2,10},{6,14},... | collective-permute-start | bytes 392 | tf_op jit(solution)/shard_map/ppermute | solution.py:37
  15.7 7.0 %collective-permute-start.2 = (bf16[2,64,576]{2,1,0:T(8,128)(2,1)S(1)}, bf16[2,64,576]{2,1,0:T(8,128)(2,1)S(1)}, u32[]{:S(2)}, u32[]{:S(2)}) collective-permute-start(bf16[2,64,576]{2,1,0:T(8,128)(2,1)S(1)} %get-tuple-element.10), channel_id=1, source_target_pairs={{0,4},{4,0},{8,12},{12,8},{1,5},{5,1},{9,13},{13,9},{2,6},{6,2},{1... | collective-permute-start | bytes 442376 | tf_op jit(solution)/shard_map/ppermute | solution.py:37
  17.3 13.9 %collective-permute-start.3 = (bf16[2,64,576]{2,1,0:T(8,128)(2,1)S(1)}, bf16[2,64,576]{2,1,0:T(8,128)(2,1)S(1)}, u32[]{:S(2)}, u32[]{:S(2)}) collective-permute-start(bf16[2,64,576]{2,1,0:T(8,128)(2,1)S(1)} %get-tuple-element.11), channel_id=1, source_target_pairs={{0,8},{4,12},{8,0},{12,4},{1,9},{5,13},{9,1},{13,5},{2,10},{6,14},... | collective-permute-start | bytes 442376 | tf_op jit(solution)/shard_map/ppermute | solution.py:37
  19.9 11.4 %collective-permute-start.4 = (bf16[2,64,576]{2,1,0:T(8,128)(2,1)S(1)}, bf16[2,64,576]{2,1,0:T(8,128)(2,1)S(1)}, u32[]{:S(2)}, u32[]{:S(2)}) collective-permute-start(bf16[2,64,576]{2,1,0:T(8,128)(2,1)S(1)} %get-tuple-element.12), channel_id=1, source_target_pairs={{0,12},{4,8},{8,4},{12,0},{1,13},{5,9},{9,5},{13,1},{2,14},{6,10},... | collective-permute-start | bytes 442376 | tf_op jit(solution)/shard_map/ppermute | solution.py:37
  22.7 10.4 %collective-permute-start.5 = (bf16[2,64,576]{2,1,0:T(8,128)(2,1)S(1)}, bf16[2,64,576]{2,1,0:T(8,128)(2,1)S(1)}, u32[]{:S(2)}, u32[]{:S(2)}) collective-permute-start(bf16[2,64,576]{2,1,0:T(8,128)(2,1)S(1)} %get-tuple-element.9.refs_0_), channel_id=1, source_target_pairs={{0,1},{1,0},{2,3},{3,2},{4,5},{5,4},{6,7},{7,6},{8,9},{9,8},{10,11... | collective-permute-start | bytes 442376 | tf_op jit(solution)/shard_map/ppermute | solution.py:37
  31.3 13.3 %collective-permute-start.12 = (bf16[16,128,128]{2,1,0:T(8,128)(2,1)S(1)}, bf16[16,128,128]{2,1,0:T(8,128)(2,1)S(1)}, u32[]{:S(2)}, u32[]{:S(2)}) collective-permute-start(bf16[16,128,128]{2,1,0:T(8,128)(2,1)S(1)} %get-tuple-element.13), channel_id=1, source_target_pairs={{0,3},{1,2},{2,1},{3,0},{16,18},{17,19},{18,16},{19,17},{4,7},{5,6... | collective-permute-start | bytes 1572872 | tf_op jit(solution)/shard_map/ppermute | solution.py:37
  31.3 14.5 %collective-permute-start.11 = (bf16[16,128,128]{2,1,0:T(8,128)(2,1)S(1)}, bf16[16,128,128]{2,1,0:T(8,128)(2,1)S(1)}, u32[]{:S(2)}, u32[]{:S(2)}) collective-permute-start(bf16[16,128,128]{2,1,0:T(8,128)(2,1)S(1)} %collective-permute-done.9.refs_9_), channel_id=1, source_target_pairs={{0,4},{4,0},{8,12},{12,8},{1,5},{5,1},{9,13},{13,9},{2,6},{6,2},{1... | collective-permute-start | bytes 1572872 | tf_op jit(solution)/shard_map/ppermute | solution.py:37
  31.3 14.5 %collective-permute-start.10 = (bf16[16,128,128]{2,1,0:T(8,128)(2,1)S(1)}, bf16[16,128,128]{2,1,0:T(8,128)(2,1)S(1)}, u32[]{:S(2)}, u32[]{:S(2)}) collective-permute-start(bf16[16,128,128]{2,1,0:T(8,128)(2,1)S(1)} %collective-permute-done.9.refs_9_), channel_id=1, source_target_pairs={{0,16},{16,0},{1,17},{17,1},{2,18},{18,2},{3,19},{19,3},{4,20},{20... | collective-permute-start | bytes 1572872 | tf_op jit(solution)/shard_map/ppermute | solution.py:37
  33.1 1.4 %collective-permute-start.6 = (bf16[2,64,576]{2,1,0:T(8,128)(2,1)S(1)}, bf16[2,64,576]{2,1,0:T(8,128)(2,1)S(1)}, u32[]{:S(2)}, u32[]{:S(2)}) collective-permute-start(bf16[2,64,576]{2,1,0:T(8,128)(2,1)S(1)} %collective-permute-done.2.refs_1_), channel_id=1, source_target_pairs={{0,1},{1,0},{2,3},{3,2},{4,5},{5,4},{6,7},{7,6},{8,9},{9,8},{10,11... | collective-permute-start | bytes 442376 | tf_op jit(solution)/shard_map/ppermute | solution.py:37
  34.5 1.4 %collective-permute-start.7 = (bf16[2,64,576]{2,1,0:T(8,128)(2,1)S(1)}, bf16[2,64,576]{2,1,0:T(8,128)(2,1)S(1)}, u32[]{:S(2)}, u32[]{:S(2)}) collective-permute-start(bf16[2,64,576]{2,1,0:T(8,128)(2,1)S(1)} %collective-permute-done.3.refs_2_), channel_id=1, source_target_pairs={{0,1},{1,0},{2,3},{3,2},{4,5},{5,4},{6,7},{7,6},{8,9},{9,8},{10,11... | collective-permute-start | bytes 442376 | tf_op jit(solution)/shard_map/ppermute | solution.py:37
  35.9 2.8 %collective-permute-start.8 = (bf16[2,64,576]{2,1,0:T(8,128)(2,1)S(1)}, bf16[2,64,576]{2,1,0:T(8,128)(2,1)S(1)}, u32[]{:S(2)}, u32[]{:S(2)}) collective-permute-start(bf16[2,64,576]{2,1,0:T(8,128)(2,1)S(1)} %collective-permute-done.4.refs_3_), channel_id=1, source_target_pairs={{0,1},{1,0},{2,3},{3,2},{4,5},{5,4},{6,7},{7,6},{8,9},{9,8},{10,11... | collective-permute-start | bytes 442376 | tf_op jit(solution)/shard_map/ppermute | solution.py:37
